TPU v7x, 256 devices: a whole 4x4x8 slice. The times are simulated.
256 devices in a mesh: ctx: 32 (over z, x_lo, core), mp: 8 (over y, x_hi).
Axes of the slice: x: 4 (x_hi: 2, x_lo: 2; x = x_hi * 2 + x_lo), y: 4, z: 8, core: 2. Of those that a mesh axis runs over, the one named last changes fastest.
Arguments:
- byte_qkv: bfloat16 [16384, 3, 4096], P('ctx', None, 'mp'), may hold values from -14 to 14
- kv_weight: bfloat16 [4096, 2, 4096], P(None, None, 'mp'), may hold values from -4 to 4
- patch_bounds: int32 [32, 161], replicated, may hold values from 0 to 16384, as said below
Outputs:
- mixed: bfloat16 [5120, 4096], P('ctx', 'mp')
Inputs may be any that keep to these rules, and one draw needn't show every extreme that they name: `patch_bounds`: row c lists in increasing order the first bytes of the patches that begin in bytes c * 512 to (c + 1) * 512 - 1, then the end of its last patch, repeated to the end of the row. The patches cover all 16384 bytes, each is 1 to 16 bytes long, one is exactly 16 long, and some row lists exactly 160 patches.
All inputs are finite; a program needn't handle non-finite values.
Results may differ from a plain program's by a relative error of at most 0.002.
The roundings to bfloat16 on the way count: a program that leaves them out, or rounds other values in their place, can miss the bound.
Values may be sent and summed in bfloat16 or wider, within the bound.
A program may use at most 128 MiB of HBM per device.

v0:
```python
import math
import jax
import jax.numpy as jnp
from jax import lax
from jax.sharding import PartitionSpec as P

D = 4096
HEADS = 32
WIN = 16
masked_score = -1e30


def passed_along(value, axis, steps):
    count = lax.axis_size(axis)
    initial, last = (max(0, -steps), min(count, count - steps))
    return lax.ppermute(value, axis, [(source, source + steps) for source in range(initial, last)])


def shards(byte_qkv, kv_weight, patch_bounds):
    byte_rows = byte_qkv.shape[0]
    col_width = byte_qkv.shape[2]
    head_dim = D // HEADS
    heads_here = col_width // head_dim
    slot_count = patch_bounds.shape[1] - 1
    score_scale = 1.0 / math.sqrt(head_dim)
    ctx_place = lax.axis_index("ctx")
    my_bounds = lax.dynamic_index_in_dim(patch_bounds, ctx_place, 0, keepdims=False)
    starts = my_bounds[:slot_count]
    lengths = my_bounds[1:] - starts
    live_slot = lengths > 0
    edge_rows = passed_along(byte_qkv[:WIN], "ctx", -1)
    extended = jnp.concatenate([byte_qkv, edge_rows], axis=0)
    offsets = jnp.arange(WIN, dtype=jnp.int32)
    local_start = jnp.clip(starts - ctx_place * byte_rows, 0, byte_rows)
    window = extended[local_start[:, None] + offsets[None, :]]
    window = window.reshape(slot_count, WIN, 3, heads_here, head_dim)
    inside = offsets[None, :] < lengths[:, None]
    queries = jnp.max(jnp.where(inside[:, :, None, None], window[:, :, 0], -jnp.inf), axis=1)
    queries = jnp.where(live_slot[:, None, None], queries, 0)
    scores = (
        jnp.einsum("shd,swhd->shw", queries, window[:, :, 1], preferred_element_type=jnp.float32)
        * score_scale
    )
    scores = jnp.where(inside[:, None, :], scores, masked_score)
    scores = scores - jnp.max(scores, axis=2, keepdims=True)
    exp_terms = jnp.exp(scores)
    weights = (exp_terms / jnp.sum(exp_terms, axis=2, keepdims=True)).astype(jnp.bfloat16)
    pooled = jnp.einsum(
        "shw,swhd->shd", weights, window[:, :, 2], preferred_element_type=jnp.float32
    )
    patch_state = (
        jnp.where(live_slot[:, None, None], pooled, 0.0)
        .astype(jnp.bfloat16)
        .reshape(slot_count, col_width)
    )
    flat_weight = kv_weight.reshape(kv_weight.shape[0], 2 * col_width)
    projected = jnp.dot(
        lax.all_gather(patch_state, "mp", axis=1, tiled=True),
        flat_weight,
        preferred_element_type=jnp.float32,
    )
    key_value = projected.astype(jnp.bfloat16)
    query_heads = patch_state.reshape(slot_count, heads_here, head_dim)
    query_slot = ctx_place * slot_count + jnp.arange(slot_count, dtype=jnp.int32)
    valid_all = (patch_bounds[:, 1:] > patch_bounds[:, :-1]).reshape(-1)
    shard_piece = lax.all_gather(key_value, "ctx", axis=0, tiled=True)
    top_score = jnp.full((heads_here, slot_count), masked_score, jnp.float32)
    piece_rows = shard_piece.shape[0]
    key_part = shard_piece[:, :col_width].reshape(piece_rows, heads_here, head_dim)
    value_part = shard_piece[:, col_width:].reshape(piece_rows, heads_here, head_dim)
    key_slot = jnp.arange(piece_rows, dtype=jnp.int32)
    visible = (key_slot[None, :] <= query_slot[:, None]) & valid_all[None, :]
    global_scores = (
        jnp.einsum("qhd,khd->hqk", query_heads, key_part, preferred_element_type=jnp.float32)
        * score_scale
    )
    global_scores = jnp.where(visible[None], global_scores, masked_score)
    new_top = jnp.maximum(top_score, jnp.max(global_scores, axis=2))
    exp_part = jnp.where(visible[None], jnp.exp(global_scores - new_top[:, :, None]), 0.0)
    denom_sum = jnp.sum(exp_part, axis=2)
    weighted = jnp.einsum(
        "hqk,khd->hqd", exp_part, value_part.astype(jnp.float32), precision=lax.Precision.HIGHEST
    )
    fold_state = (new_top, denom_sum, weighted)
    top_score, denom_sum, weighted = fold_state
    safe_total = jnp.where(denom_sum > 0, denom_sum, 1.0)
    attended = (weighted / safe_total[:, :, None]).transpose(1, 0, 2).reshape(slot_count, col_width)
    attended = jnp.where(live_slot[:, None], attended, 0.0)
    return (patch_state.astype(jnp.float32) + attended).astype(jnp.bfloat16)


def solution(mesh):
    return jax.shard_map(
        shards,
        mesh=mesh,
        in_specs=(P("ctx", None, "mp"), P(None, None, "mp"), P()),
        out_specs=P("ctx", "mp"),
        check_vma=False,
    )
```

profile of v0, /device:TPU:1, one launch (start us, length us, event | category | flops | bytes accessed | tf_op | source)
XLA Modules:
  0.0 252.5 jit_solution(9994078554285454188)
XLA Ops:
  6.5 0.0 all-gather.3.cloned.1.call-start
  6.5 2.8 %copy.29 = bf16[512,3,512]{2,1,0:T(4,128)(2,1)S(1)} copy(bf16[512,3,512]{2,0,1:T(8,128)(2,1)} %param.3) | data formatting | bytes 3145728 | tf_op args[0]
  9.3 0.0 copy-start
  9.3 1.3 copy-done
  10.7 5.1 %collective-permute-start = (bf16[16,3,512]{2,1,0:T(4,128)(2,1)S(1)}, bf16[16,3,512]{2,1,0:T(4,128)(2,1)S(1)}, u32[]{:S(2)}, u32[]{:S(2)}) collective-permute-start(bf16[16,3,512]{2,1,0:T(4,128)(2,1)S(1)} %slice.44), channel_id=1, source_target_pairs={{8,0},{16,8},{24,16},{32,24},{40,32},{48,40},{56,48},{64,56},{72,6... | collective-permute-start | bytes 147464 | tf_op jit(solution)/shard_map/ppermute | solution.py:16
  15.8 0.9 dynamic-slice_subtract_fusion
  16.7 0.1 iota_compare_fusion.1
  16.8 0.1 compare_select_fusion
  16.9 0.1 reshape.193
  17.0 0.1 copy.27
  17.0 0.1 collective-permute-done
  17.1 3.0 %pad_maximum_fusion = bf16[528,3,512]{2,1,0:T(4,128)(2,1)S(1)} fusion(bf16[16,3,512]{2,1,0:T(4,128)(2,1)S(1)} %collective-permute-done, bf16[512,3,512]{2,1,0:T(4,128)(2,1)} %copy-done), kind=kLoop, calls=%fused_computation.31 | loop fusion | flops 811008 | bytes 3244032 | tf_op jit(solution)/shard_map/concatenate | solution.py:32
  20.1 12.8 %gather_fusion = bf16[2560,3,512]{2,1,0:T(4,128)(2,1)} fusion(bf16[528,3,512]{2,1,0:T(4,128)(2,1)S(1)} %pad_maximum_fusion, s32[3072]{0:T(1024)S(1)} %pad_clamp_fusion), kind=kCustom, calls=%fused_computation | custom fusion | bytes 15738880 | tf_op jit(solution)/shard_map/gather | solution.py:35
  33.0 21.7 %reshape.205 = bf16[160,16,3,4,128]{4,3,2,1,0:T(4,128)(2,1)} reshape(bf16[2560,3,512]{2,1,0:T(4,128)(2,1)} %gather_fusion) | data formatting | bytes 15728640 | tf_op jit(solution)/shard_map/reshape | solution.py:36
  54.6 5.4 %fusion.17 = bf16[160,4,128]{2,1,0:T(4,128)(2,1)S(1)} fusion(bf16[160,16,3,4,128]{4,3,2,1,0:T(4,128)(2,1)} %reshape.205, pred[160,16]{1,0:T(8,128)(4,1)S(1)} %iota_compare_fusion.1), kind=kLoop, calls=%fused_computation.26 | loop fusion | flops 2539520 | bytes 2787840 | tf_op jit(solution)/shard_map/reduce_max | solution.py:38
  60.0 5.2 %slice_bitcast_fusion.2 = (bf16[160,16,4,128]{3,2,1,0:T(4,128)(2,1)S(1)}, bf16[160,16,4,128]{3,2,1,0:T(4,128)(2,1)S(1)}) fusion(bf16[160,16,3,4,128]{4,3,2,1,0:T(4,128)(2,1)} %reshape.205), kind=kLoop, calls=%fused_computation.22 | loop fusion | bytes 10485760 | tf_op jit(solution)/shard_map/squeeze | solution.py:49
  65.1 0.2 select_bitcast_fusion
  65.4 1.4 fusion.20
  66.8 0.2 copy.37
  67.0 0.1 fusion.29
  67.1 0.2 copy.38
  67.3 0.8 fusion.18
  68.1 0.2 select_convert_fusion
  68.4 0.7 copy.80
  69.1 0.0 all-gather.3.cloned.1.call-update
  69.1 0.2 all-gather.5.cloned.1.call-start
  69.3 9.3 %copy.49 = bf16[512,8,2,512]{3,1,2,0:T(8,128)(2,1)} copy(bf16[512,8,2,512]{3,2,1,0:T(2,128)(2,1)} %bitcast.80) | data formatting | bytes 16777216
  78.6 44.9 %all-gather.3.cloned.1.call-done = bf16[160,4096]{1,0:T(8,128)(2,1)} async-done(((bf16[160,512]{1,0:T(8,128)(2,1)}), bf16[160,4096]{1,0:T(8,128)(2,1)}) %all-gather.3.cloned.1.call-update) | async-done | bytes 1310736 | tf_op jit(solution)/shard_map/all_gather | solution.py:58
  123.5 0.0 copy-start.1
  123.5 6.1 %convolution_convert_fusion = bf16[160,1024]{1,0:T(8,128)(2,1)} fusion(bf16[160,4096]{1,0:T(8,128)(2,1)} %all-gather.3.cloned.1.call-done, bf16[4096,1024]{1,0:T(8,128)(2,1)} %bitcast.81), kind=kOutput, calls=%fused_computation.32 | convolution fusion | flops 1342341120 | bytes 10027008 | tf_op jit(solution)/shard_map/dot_general | solution.py:57
  129.6 0.0 all-gather.5.cloned.1.call-update
  129.6 0.0 copy-done.1
  129.6 0.1 slice_compare_fusion
  129.7 0.1 and.15
  129.8 0.6 fusion.15
  130.4 73.0 %all-gather.5.cloned.1.call-done = bf16[5120,1024]{1,0:T(8,128)(2,1)} async-done(((bf16[160,1024]{1,0:T(8,128)(2,1)}), bf16[5120,1024]{1,0:T(8,128)(2,1)}) %all-gather.5.cloned.1.call-update) | async-done | bytes 10485776 | tf_op jit(solution)/shard_map/all_gather | solution.py:66
  203.4 9.7 %slice_bitcast_fusion.1 = (bf16[640,4,8,128]{3,2,1,0:T(8,128)(2,1)}, bf16[640,4,8,128]{3,2,1,0:T(8,128)(2,1)}) fusion(bf16[5120,1024]{1,0:T(8,128)(2,1)} %all-gather.5.cloned.1.call-done), kind=kLoop, calls=%fused_computation.19 | loop fusion | bytes 20971520
  213.1 10.3 %fusion.2 = (f32[4,160]{1,0:T(4,128)S(1)}, f32[4,160,5120]{2,1,0:T(8,128)}) fusion(pred[160,5120]{1,0:T(8,128)(4,1)S(1)} %fusion.15, bf16[640,4,8,128]{3,2,1,0:T(8,128)(2,1)} %get-tuple-element.5, bf16[160,4,128]{2,1,0:T(4,128)(2,1)S(1)} %select_convert_fusion), kind=kOutput, calls=%fused_computation.5 | convolution fusion | flops 848690560 | bytes 19335680 | tf_op jit(solution)/shard_map/qhd,khd->hqk/dot_general | solution.py:74
  223.4 8.8 %fusion.3 = f32[4,160]{1,0:T(4,128)S(1)} fusion(f32[4,160,5120]{2,1,0:T(8,128)} %get-tuple-element.12, f32[4,160]{1,0:T(4,128)S(1)} %broadcast_maximum_fusion, pred[160,5120]{1,0:T(8,128)(4,1)S(1)} %fusion.15), kind=kLoop, calls=%fused_computation.6 | loop fusion | flops 16383360 | bytes 13931520 | tf_op jit(solution)/shard_map/reduce_sum | solution.py:80
  232.3 12.6 %fusion.33 = f32[4,20,8,128]{3,2,1,0:T(8,128)S(1)} fusion(bf16[640,4,8,128]{3,2,1,0:T(8,128)(2,1)} %get-tuple-element.6, f32[4,160,5120]{2,1,0:T(8,128)} %get-tuple-element.12, f32[4,160]{1,0:T(4,128)S(1)} %broadcast_maximum_fusion, pred[160,5120]{1,0:T(8,128)(4,1)S(1)} %fusion.15, f32[160,4]{0,1:T(4,128)S(1)} %compare_select_fusion.1), kind=kOutput, calls=%fused_computation.40 | convolution fusion | flops 5046353920 | bytes 19502080 | tf_op jit(solution)/shard_map/hqk,khd->hqd/dot_general | solution.py:81
  244.9 0.8 fusion.37
  (6 shorter events, 0.1 us)
Async XLA Ops:
  6.5 117.0 %all-gather.3.cloned.1.call-start = ((), (), s32[]{:S(2)}) async-start(), calls=%async_computation | async-start | bytes 1474560 | tf_op jit(solution)/shard_map/all_gather | solution.py:58
  9.3 1.4 copy-start
  10.7 6.4 %collective-permute-start = (bf16[16,3,512]{2,1,0:T(4,128)(2,1)S(1)}, bf16[16,3,512]{2,1,0:T(4,128)(2,1)S(1)}, u32[]{:S(2)}, u32[]{:S(2)}) collective-permute-start(bf16[16,3,512]{2,1,0:T(4,128)(2,1)S(1)} %slice.44), channel_id=1, source_target_pairs={{8,0},{16,8},{24,16},{32,24},{40,32},{48,40},{56,48},{64,56},{72,6... | collective-permute-start | bytes 147464 | tf_op jit(solution)/shard_map/ppermute | solution.py:16
  69.1 134.3 %all-gather.5.cloned.1.call-start = ((), (), s32[]{:S(2)}) async-start(), calls=%async_computation.1 | async-start | bytes 10813440 | tf_op jit(solution)/shard_map/all_gather | solution.py:66
  123.5 6.1 %copy-start.1 = (s32[32,161]{1,0:T(8,128)S(1)}, s32[32,161]{1,0:T(8,128)}, u32[]{:S(2)}) copy-start(s32[32,161]{1,0:T(8,128)} %param.5) | copy-start | bytes 61828
Sparse Core Ops, SparseCore 0:
  69.2 54.2 all-gather.2
  129.7 73.6 all-gather.4
where the time goes:
time: 253 us
  waiting for transfers between devices  118 us (47%)
  local copies, waits for them, and re-layouts  64.2 us (25%)
  matrix products  31.2 us (12%)
  other arithmetic  20.3 us (8%)
  between operations  13.6 us (5%)
  starting transfers between devices  5.33 us (2%)
    all_gather x1, waiting for transfers between devices, shards(): shard_piece = lax.all_gather(key_value, 'ctx', axis=0, tiled=True)  73 us
    all_gather x1, waiting for transfers between devices, shards(): lax.all_gather(patch_state, 'mp', axis=1, tiled=True)  44.9 us
    unnamed x8, local copies, waits for them, and re-layouts  23.8 us
    reshape x1, local copies, waits for them, and re-layouts, shards(): window = window.reshape(slot_count, WIN, 3, heads_here, head_dim)  21.7 us
    gather x1, local copies, waits for them, and re-layouts, shards(): window = extended[local_start[:, None] + offsets[None, :]]  12.8 us
    dot_general x1, matrix products, shards(): jnp.einsum('hqk,khd->hqd', exp_part, value_part.astype(jnp.float32), prec...  12.6 us
    dot_general x1, matrix products, shards(): jnp.einsum('qhd,khd->hqk', query_heads, key_part, preferred_element_type=...  10.3 us
    reduce_sum x1, other arithmetic, shards(): denom_sum = jnp.sum(exp_part, axis=2)  8.85 us
  transfers between devices with their start and end apart: 3, of which 3 were waited for; matrix products, arithmetic and copies ran while one was open for 4% of the time, Pallas kernels for 0%

commit v1 on v0

--- a/solution.py
+++ b/solution.py
@@ -1,3 +1,4 @@
+import functools
 import math
 import jax
 import jax.numpy as jnp
@@ -8,6 +9,21 @@
 HEADS = 32
 WIN = 16
 masked_score = -1e30
+
+
+def name_columns(obj, dim_k):
+    return jnp.concatenate(
+        lax.all_to_all(
+            jnp.stack([obj for _ in range(lax.axis_size("mp"))], 0),
+            split_axis=0,
+            concat_axis=0,
+            axis_name="mp",
+        ),
+        dim_k,
+    )
+
+
+assign_sizes = functools.partial(name_columns, dim_k=1)
 
 
 def passed_along(value, axis, steps):
@@ -54,11 +70,7 @@
         .reshape(slot_count, col_width)
     )
     flat_weight = kv_weight.reshape(kv_weight.shape[0], 2 * col_width)
-    projected = jnp.dot(
-        lax.all_gather(patch_state, "mp", axis=1, tiled=True),
-        flat_weight,
-        preferred_element_type=jnp.float32,
-    )
+    projected = jnp.dot(assign_sizes(patch_state), flat_weight, preferred_element_type=jnp.float32)
     key_value = projected.astype(jnp.bfloat16)
     query_heads = patch_state.reshape(slot_count, heads_here, head_dim)
     query_slot = ctx_place * slot_count + jnp.arange(slot_count, dtype=jnp.int32)

time: 253 us -> 226 us (0.89)
  waiting for transfers between devices: 118 us -> 83.4 us
  starting transfers between devices: 5.33 us -> 11.9 us
    all_gather x1 -> x0, waiting for transfers between devices: 44.9 us -> none  [shards(): lax.all_gather(patch_state, 'mp', axis=1, tiled=True)]
    all_to_all x0 -> x1, waiting for transfers between devices: none -> 9.75 us  [name_columns(): lax.all_to_all(jnp.stack([obj for _ in range(lax.axis_size('mp'))], 0), s...]
    all_to_all x0 -> x1, starting transfers between devices: none -> 6.61 us  [name_columns(): lax.all_to_all(jnp.stack([obj for _ in range(lax.axis_size('mp'))], 0), s...]
  transfers between devices with their start and end apart: 3 -> 3, of which waited for: 3 -> 3; matrix products, arithmetic and copies ran while one was open for 4% -> 5% of each run, Pallas kernels for 0% -> 0%
where the time goes in v1:
time: 226 us; the launch traced here: 225 us
  waiting for transfers between devices  83.4 us (37%)
  local copies, waits for them, and re-layouts  64.9 us (29%)
  matrix products  30.9 us (14%)
  other arithmetic  20.3 us (9%)
  between operations  13.6 us (6%)
  starting transfers between devices  11.9 us (5%)
    all_gather x1, waiting for transfers between devices, shards(): shard_piece = lax.all_gather(key_value, 'ctx', axis=0, tiled=True)  73.6 us
    unnamed x8, local copies, waits for them, and re-layouts  23.2 us
    reshape x1, local copies, waits for them, and re-layouts, shards(): window = window.reshape(slot_count, WIN, 3, heads_here, head_dim)  21.7 us
    gather x1, local copies, waits for them, and re-layouts, shards(): window = extended[local_start[:, None] + offsets[None, :]]  12.8 us
    dot_general x1, matrix products, shards(): jnp.einsum('hqk,khd->hqd', exp_part, value_part.astype(jnp.float32), prec...  12.6 us
    dot_general x1, matrix products, shards(): jnp.einsum('qhd,khd->hqk', query_heads, key_part, preferred_element_type=...  10.3 us
    all_to_all x1, waiting for transfers between devices, name_columns(): lax.all_to_all(jnp.stack([obj for _ in range(lax.axis_size('mp'))], 0), s...  9.75 us
    reduce_sum x1, other arithmetic, shards(): denom_sum = jnp.sum(exp_part, axis=2)  8.85 us
  transfers between devices with their start and end apart: 3, of which 3 were waited for; matrix products, arithmetic and copies ran while one was open for 5% of the time, Pallas kernels for 0%

profile of v1, /device:TPU:1, one launch (start us, length us, event | category | flops | bytes accessed | tf_op | source)
XLA Modules:
  0.0 225.0 jit_solution(13234942373259320749)
XLA Ops:
  6.5 2.8 %copy.30 = bf16[512,3,512]{2,1,0:T(4,128)(2,1)S(1)} copy(bf16[512,3,512]{2,0,1:T(8,128)(2,1)} %param.3) | data formatting | bytes 3145728 | tf_op args[0]
  9.3 0.0 copy-start
  9.3 1.3 copy-done
  10.7 5.1 %collective-permute-start = (bf16[16,3,512]{2,1,0:T(4,128)(2,1)S(1)}, bf16[16,3,512]{2,1,0:T(4,128)(2,1)S(1)}, u32[]{:S(2)}, u32[]{:S(2)}) collective-permute-start(bf16[16,3,512]{2,1,0:T(4,128)(2,1)S(1)} %slice.44), channel_id=1, source_target_pairs={{8,0},{16,8},{24,16},{32,24},{40,32},{48,40},{56,48},{64,56},{72,6... | collective-permute-start | bytes 147464 | tf_op jit(solution)/shard_map/ppermute | solution.py:32
  15.8 0.9 dynamic-slice_subtract_fusion
  16.7 0.1 iota_compare_fusion.1
  16.8 0.1 compare_select_fusion
  16.8 0.1 reshape.203
  17.0 0.1 copy.28
  17.0 0.1 collective-permute-done
  17.1 3.0 %pad_maximum_fusion = bf16[528,3,512]{2,1,0:T(4,128)(2,1)S(1)} fusion(bf16[16,3,512]{2,1,0:T(4,128)(2,1)S(1)} %collective-permute-done, bf16[512,3,512]{2,1,0:T(4,128)(2,1)} %copy-done), kind=kLoop, calls=%fused_computation.31 | loop fusion | flops 811008 | bytes 3244032 | tf_op jit(solution)/shard_map/concatenate | solution.py:48
  20.1 12.8 %gather_fusion = bf16[2560,3,512]{2,1,0:T(4,128)(2,1)} fusion(bf16[528,3,512]{2,1,0:T(4,128)(2,1)S(1)} %pad_maximum_fusion, s32[3072]{0:T(1024)S(1)} %pad_clamp_fusion), kind=kCustom, calls=%fused_computation | custom fusion | bytes 15738880 | tf_op jit(solution)/shard_map/gather | solution.py:51
  33.0 21.7 %reshape.215 = bf16[160,16,3,4,128]{4,3,2,1,0:T(4,128)(2,1)} reshape(bf16[2560,3,512]{2,1,0:T(4,128)(2,1)} %gather_fusion) | data formatting | bytes 15728640 | tf_op jit(solution)/shard_map/reshape | solution.py:52
  54.6 5.4 %fusion.17 = bf16[160,4,128]{2,1,0:T(4,128)(2,1)S(1)} fusion(bf16[160,16,3,4,128]{4,3,2,1,0:T(4,128)(2,1)} %reshape.215, pred[160,16]{1,0:T(8,128)(4,1)S(1)} %iota_compare_fusion.1), kind=kLoop, calls=%fused_computation.26 | loop fusion | flops 2539520 | bytes 2787840 | tf_op jit(solution)/shard_map/reduce_max | solution.py:54
  60.0 5.2 %slice_bitcast_fusion.2 = (bf16[160,16,4,128]{3,2,1,0:T(4,128)(2,1)S(1)}, bf16[160,16,4,128]{3,2,1,0:T(4,128)(2,1)S(1)}) fusion(bf16[160,16,3,4,128]{4,3,2,1,0:T(4,128)(2,1)} %reshape.215), kind=kLoop, calls=%fused_computation.22 | loop fusion | bytes 10485760 | tf_op jit(solution)/shard_map/squeeze | solution.py:65
  65.1 0.2 select_bitcast_fusion
  65.4 1.4 fusion.20
  66.8 0.2 copy.39
  67.0 0.1 fusion.29
  67.1 0.2 copy.40
  67.3 0.8 fusion.18
  68.1 0.2 select_convert_fusion
  68.4 1.3 stack.3
  69.7 6.6 %all-to-all-start = ((bf16[8,160,512]{2,1,0:T(8,128)(2,1)}), bf16[8,160,512]{2,1,0:T(8,128)(2,1)S(1)}, u32[]{:S(2)}, u32[]{:S(2)}) async-start(bf16[8,160,512]{2,1,0:T(8,128)(2,1)} %stack.3), calls=%async_computation | async-start | bytes 2621440 | tf_op jit(solution)/shard_map/all_to_all | solution.py:16
  76.3 0.2 all-gather.2.cloned.1.call-start
  76.5 9.3 %copy.52 = bf16[512,8,2,512]{3,1,2,0:T(8,128)(2,1)} copy(bf16[512,8,2,512]{3,2,1,0:T(2,128)(2,1)} %bitcast.83) | data formatting | bytes 16777216
  85.8 9.8 %all-to-all-done = bf16[8,160,512]{2,1,0:T(8,128)(2,1)S(1)} async-done(((bf16[8,160,512]{2,1,0:T(8,128)(2,1)}), bf16[8,160,512]{2,1,0:T(8,128)(2,1)S(1)}, u32[]{:S(2)}, u32[]{:S(2)}) %all-to-all-start) | async-done | bytes 1310752 | tf_op jit(solution)/shard_map/all_to_all | solution.py:16
  95.6 0.1 copy.49
  95.7 0.0 copy-start.1
  95.7 5.7 %convolution_convert_fusion = bf16[160,1024]{1,0:T(8,128)(2,1)} fusion(bf16[160,4096]{1,0:T(8,128)(2,1)S(1)} %bitcast.88, bf16[4096,1024]{1,0:T(8,128)(2,1)} %bitcast.84), kind=kOutput, calls=%fused_computation.32 | convolution fusion | flops 1342341120 | bytes 10027008 | tf_op jit(solution)/shard_map/dot_general | solution.py:73
  101.4 0.0 all-gather.2.cloned.1.call-update
  101.5 0.0 copy-done.1
  101.5 0.1 slice_compare_fusion
  101.5 0.1 and.15
  101.7 0.6 fusion.15
  102.3 73.6 %all-gather.2.cloned.1.call-done = bf16[5120,1024]{1,0:T(8,128)(2,1)} async-done(((bf16[160,1024]{1,0:T(8,128)(2,1)}), bf16[5120,1024]{1,0:T(8,128)(2,1)}) %all-gather.2.cloned.1.call-update) | async-done | bytes 10485776 | tf_op jit(solution)/shard_map/all_gather | solution.py:78
  175.8 9.7 %slice_bitcast_fusion.1 = (bf16[640,4,8,128]{3,2,1,0:T(8,128)(2,1)}, bf16[640,4,8,128]{3,2,1,0:T(8,128)(2,1)}) fusion(bf16[5120,1024]{1,0:T(8,128)(2,1)} %all-gather.2.cloned.1.call-done), kind=kLoop, calls=%fused_computation.19 | loop fusion | bytes 20971520
  185.6 10.3 %fusion.2 = (f32[4,160]{1,0:T(4,128)S(1)}, f32[4,160,5120]{2,1,0:T(8,128)}) fusion(pred[160,5120]{1,0:T(8,128)(4,1)S(1)} %fusion.15, bf16[640,4,8,128]{3,2,1,0:T(8,128)(2,1)} %get-tuple-element.5, bf16[160,4,128]{2,1,0:T(4,128)(2,1)S(1)} %select_convert_fusion), kind=kOutput, calls=%fused_computation.5 | convolution fusion | flops 848690560 | bytes 19335680 | tf_op jit(solution)/shard_map/qhd,khd->hqk/dot_general | solution.py:86
  195.9 8.8 %fusion.3 = f32[4,160]{1,0:T(4,128)S(1)} fusion(f32[4,160,5120]{2,1,0:T(8,128)} %get-tuple-element.12, f32[4,160]{1,0:T(4,128)S(1)} %broadcast_maximum_fusion, pred[160,5120]{1,0:T(8,128)(4,1)S(1)} %fusion.15), kind=kLoop, calls=%fused_computation.6 | loop fusion | flops 16383360 | bytes 13931520 | tf_op jit(solution)/shard_map/reduce_sum | solution.py:92
  204.7 12.6 %fusion.33 = f32[4,20,8,128]{3,2,1,0:T(8,128)S(1)} fusion(bf16[640,4,8,128]{3,2,1,0:T(8,128)(2,1)} %get-tuple-element.6, f32[4,160,5120]{2,1,0:T(8,128)} %get-tuple-element.12, f32[4,160]{1,0:T(4,128)S(1)} %broadcast_maximum_fusion, pred[160,5120]{1,0:T(8,128)(4,1)S(1)} %fusion.15, f32[160,4]{0,1:T(4,128)S(1)} %compare_select_fusion.1), kind=kOutput, calls=%fused_computation.40 | convolution fusion | flops 5046353920 | bytes 19502080 | tf_op jit(solution)/shard_map/hqk,khd->hqd/dot_general | solution.py:93
  217.4 0.8 fusion.37
  (7 shorter events, 0.1 us)
Async XLA Ops:
  9.3 1.4 copy-start
  10.7 6.4 %collective-permute-start = (bf16[16,3,512]{2,1,0:T(4,128)(2,1)S(1)}, bf16[16,3,512]{2,1,0:T(4,128)(2,1)S(1)}, u32[]{:S(2)}, u32[]{:S(2)}) collective-permute-start(bf16[16,3,512]{2,1,0:T(4,128)(2,1)S(1)} %slice.44), channel_id=1, source_target_pairs={{8,0},{16,8},{24,16},{32,24},{40,32},{48,40},{56,48},{64,56},{72,6... | collective-permute-start | bytes 147464 | tf_op jit(solution)/shard_map/ppermute | solution.py:32
  69.7 25.9 %all-to-all-start = ((bf16[8,160,512]{2,1,0:T(8,128)(2,1)}), bf16[8,160,512]{2,1,0:T(8,128)(2,1)S(1)}, u32[]{:S(2)}, u32[]{:S(2)}) async-start(bf16[8,160,512]{2,1,0:T(8,128)(2,1)} %stack.3), calls=%async_computation | async-start | bytes 2621440 | tf_op jit(solution)/shard_map/all_to_all | solution.py:16
  76.3 99.6 %all-gather.2.cloned.1.call-start = ((), (), s32[]{:S(2)}) async-start(), calls=%async_computation.1 | async-start | bytes 10813440 | tf_op jit(solution)/shard_map/all_gather | solution.py:78
  95.7 5.7 %copy-start.1 = (s32[32,161]{1,0:T(8,128)S(1)}, s32[32,161]{1,0:T(8,128)}, u32[]{:S(2)}) copy-start(s32[32,161]{1,0:T(8,128)} %param.5) | copy-start | bytes 61828
Sparse Core Ops, SparseCore 0:
  101.6 74.2 all-gather.1
